TPU v7x, 256 devices: a whole 4x4x8 slice. The times are simulated.
256 devices in a mesh: dp: 64 (over x, z, core), dim: 4 (over y).
Axes of the slice: x: 4, y: 4, z: 8, core: 2. Of those that a mesh axis runs over, the one named last changes fastest.
Arguments:
- vectors: bfloat16 [768, 65536], P('dim', 'dp'), may hold values from -30 to 30
- codes: int32 [64, 65536], P('dim', 'dp'), may hold values from 0 to 255, as said below
- codebook: bfloat16 [256, 768], P(None, 'dim'), may hold values from -4 to 4
Outputs:
- rotation: float32 [768, 768], P('dim')
- new_codebook: float32 [256, 768], P('dp', 'dim')
Inputs may be any that keep to these rules, and one draw needn't show every extreme that they name: `codes`: each entry names a centroid of its subspace; in each subspace at least one centroid, which one is drawn from the seed, is named by no vector.
All inputs are finite; a program needn't handle non-finite values.
Results may differ from a plain program's by a relative error of at most 0.003.
Values may be sent and summed in bfloat16 or wider, within the bound.
A program may use at most 64 MiB of HBM per device.

v0:
```python
import jax
import jax.numpy as jnp
from jax import lax
from jax.sharding import PartitionSpec as P

NS_STEPS = 4


def per_device(vectors, codes, codebook):
    local_width = vectors.shape[0]
    row_count = vectors.shape[1]
    sub_local = codes.shape[0]
    sub_width = local_width // sub_local
    centroid_count = codebook.shape[0]
    dp_count = lax.axis_size("dp")
    dim_count = lax.axis_size("dim")
    total_width = local_width * dim_count
    block_rows = min(512, row_count)
    block_count = row_count // block_rows
    levels = jnp.arange(centroid_count, dtype=jnp.int32)
    book_cube = codebook.reshape(centroid_count, sub_local, sub_width)
    gathered_rows = lax.all_gather(vectors, "dim", axis=0, tiled=True)

    def block_onehot(block_index):
        start = block_index * block_rows
        code_block = lax.dynamic_slice_in_dim(codes, start, block_rows, 1)
        onehot = (code_block[:, :, None] == levels[None, None, :]).astype(jnp.bfloat16)
        row_block = lax.dynamic_slice_in_dim(gathered_rows, start, block_rows, 1)
        return (onehot, row_block)

    def add_cross(block_index, cross_part):
        onehot, row_block = block_onehot(block_index)
        decoded = jnp.einsum("mnk,kmd->nmd", onehot, book_cube, preferred_element_type=jnp.float32)
        decoded = decoded.reshape(block_rows, local_width).astype(jnp.bfloat16)
        return cross_part + jnp.einsum(
            "nd,cn->dc", decoded, row_block, preferred_element_type=jnp.float32
        )

    cross_part = lax.fori_loop(
        0, block_count, add_cross, jnp.zeros((local_width, total_width), jnp.float32)
    )

    def newton_update(rows, whole):
        gram_rows = jnp.dot(rows, whole.T, precision=lax.Precision.HIGHEST)
        return 1.5 * rows - 0.5 * jnp.dot(gram_rows, whole, precision=lax.Precision.HIGHEST)

    own_rows = lax.psum_scatter(cross_part, "dp", scatter_dimension=0, tiled=True)
    thin_width = own_rows.shape[0]
    dim_index = lax.axis_index("dim")

    def gather_spread(rows):
        return lax.all_gather(rows, ("dp", "dim"), axis=0, tiled=True)

    gathered = gather_spread(own_rows)
    magnitude = jnp.sqrt(jnp.sum(gathered * gathered))
    gathered = gathered / magnitude
    own_rows = own_rows / magnitude

    def spread_step(iteration, carry):
        rows, whole = carry
        rows = newton_update(rows, whole)
        return (rows, gather_spread(rows))

    own_rows, gathered = lax.fori_loop(0, NS_STEPS - 1, spread_step, (own_rows, gathered))
    shaped = gathered.reshape(dp_count, dim_count, thin_width, total_width)
    block_part = lax.dynamic_slice_in_dim(shaped, dim_index, 1, 1).reshape(local_width, total_width)
    rotation = newton_update(block_part, gathered)
    rotation_low = rotation.astype(jnp.bfloat16)

    def add_centroids(block_index, carry):
        centroid_sums, counts = carry
        onehot, row_block = block_onehot(block_index)
        rotated = jnp.einsum(
            "cn,dc->nd", row_block, rotation_low, preferred_element_type=jnp.float32
        ).astype(jnp.bfloat16)
        rotated = rotated.reshape(block_rows, sub_local, sub_width)
        centroid_sums = centroid_sums + jnp.einsum(
            "mnk,nmd->kmd", onehot, rotated, preferred_element_type=jnp.float32
        )
        counts = counts + jnp.sum(onehot, axis=1, dtype=jnp.float32).T
        return (centroid_sums, counts)

    start_sums = jnp.zeros((centroid_count, sub_local, sub_width), jnp.float32)
    start_counts = jnp.zeros((centroid_count, sub_local), jnp.float32)
    centroid_sums, counts = lax.fori_loop(0, block_count, add_centroids, (start_sums, start_counts))
    owned_sums, owned_counts = (
        lax.psum_scatter(
            centroid_sums.reshape(centroid_count, local_width),
            "dp",
            scatter_dimension=0,
            tiled=True,
        ),
        lax.psum_scatter(counts, "dp", scatter_dimension=0, tiled=True),
    )
    divisor = jnp.repeat(jnp.maximum(owned_counts, 1.0), sub_width, axis=1)
    new_codebook = owned_sums / divisor
    return (rotation, new_codebook)


def solution(mesh):
    placed = (P("dim", "dp"), P("dim", "dp"), P(None, "dim"))
    return jax.shard_map(
        per_device,
        mesh=mesh,
        in_specs=placed,
        out_specs=(P("dim", None), P("dp", "dim")),
        check_vma=False,
    )
```

profile of v0, /device:TPU:8, one launch (start us, length us, event | category | flops | bytes accessed | tf_op | source)
XLA Modules:
  0.0 973.8 jit_solution(7501567277466070156)
XLA Ops:
  7.2 0.0 all-gather.8.cloned.1.call-start
  7.2 0.7 all-gather.8.cloned.1.call-update
  7.9 0.0 all-reduce.6.cloned.1.call-start
  8.0 0.9 reshape.36
  8.9 31.9 %all-gather.8.cloned.1.call-done = bf16[768,1024]{1,0:T(8,128)(2,1)} async-done(((bf16[192,1024]{1,0:T(8,128)(2,1)}), bf16[768,1024]{1,0:T(8,128)(2,1)}) %all-gather.8.cloned.1.call-update) | async-done | bytes 1572880 | tf_op jit(solution)/shard_map/all_gather | solution.py:22
  40.8 6.8 while.43
  40.8 0.8 constant_dynamic-slice_fusion.7
  41.5 2.0 fusion.57
  43.5 0.1 convert_element_type.62
  43.6 0.5 convolution_add_fusion.2
  44.2 0.8 constant_dynamic-slice_fusion.7
  44.9 2.0 fusion.57
  46.9 0.1 convert_element_type.62
  47.0 0.5 convolution_add_fusion.2
  47.6 0.8 copy-done.1
  48.4 0.0 all-gather.10.cloned.1.call-start
  48.5 0.6 dynamic-slice
  49.6 182.2 %all-reduce.6.cloned.1.call-done = f32[192,768]{1,0:T(8,128)} async-done(((f32[192,768]{1,0:T(8,128)}), f32[192,768]{1,0:T(8,128)}) %all-reduce.6.cloned.1.call-update) | async-done | bytes 589840
  231.8 1.4 dynamic-slice_bitcast_fusion
  233.8 106.4 %all-gather.10.cloned.1.call-done = f32[256,3,768]{2,1,0:T(4,128)} async-done(((f32[1,3,768]{2,1,0:T(4,128)}), f32[256,3,768]{2,1,0:T(4,128)}) %all-gather.10.cloned.1.call-update) | async-done | bytes 2359312 | tf_op jit(solution)/shard_map/all_gather | solution.py:52
  340.2 4.3 multiply_reduce_fusion
  345.2 2.2 broadcast_divide_fusion
  347.4 3.2 reshape.47
  350.6 0.8 dynamic-slice_divide_fusion
  351.4 337.2 %while.42 = (s32[]{:T(128)}, f32[3,768]{1,0:T(4,128)S(1)}, f32[768,768]{1,0:T(8,128)S(1)}, s32[]{:T(128)}) while((s32[]{:T(128)}, f32[3,768]{1,0:T(4,128)S(1)}, f32[768,768]{1,0:T(8,128)S(1)}, s32[]{:T(128)}) %tuple.81), condition=%wide.region_5.0_spmd, body=%wide.region_4.0_spmd.sunk | while | flops 42474240 | bytes 17452180 | solution.py:64
  351.5 2.0 fusion.52
  353.5 1.2 fusion.53
  354.7 0.6 copy-done.3
  355.4 105.2 %all-gather.12.cloned.1.call-done = f32[256,3,768]{2,1,0:T(4,128)} async-done(((f32[1,3,768]{2,1,0:T(4,128)}), f32[256,3,768]{2,1,0:T(4,128)}) %all-gather.12.cloned.1.call-update) | async-done | bytes 2359312 | tf_op jit(solution)/shard_map/while/body/eval_jaxpr/all_gather | solution.py:52
  460.6 3.2 reshape.58
  463.9 0.0 all-gather.12.cloned.1.call-start
  463.9 2.0 fusion.52
  465.9 1.2 fusion.53
  467.1 0.6 copy-done.3
  467.8 105.2 %all-gather.12.cloned.1.call-done = f32[256,3,768]{2,1,0:T(4,128)} async-done(((f32[1,3,768]{2,1,0:T(4,128)}), f32[256,3,768]{2,1,0:T(4,128)}) %all-gather.12.cloned.1.call-update) | async-done | bytes 2359312 | tf_op jit(solution)/shard_map/while/body/eval_jaxpr/all_gather | solution.py:52
  573.0 3.2 reshape.58
  576.3 0.0 all-gather.12.cloned.1.call-start
  576.3 2.0 fusion.52
  578.3 1.2 fusion.53
  579.6 0.6 copy-done.3
  580.2 105.2 %all-gather.12.cloned.1.call-done = f32[256,3,768]{2,1,0:T(4,128)} async-done(((f32[1,3,768]{2,1,0:T(4,128)}), f32[256,3,768]{2,1,0:T(4,128)}) %all-gather.12.cloned.1.call-update) | async-done | bytes 2359312 | tf_op jit(solution)/shard_map/while/body/eval_jaxpr/all_gather | solution.py:52
  685.4 3.2 reshape.58
  688.7 0.0 all-reduce.8.cloned.1.call-start
  688.7 2.6 reshape.37
  691.3 2.2 constant_dynamic-slice_fusion.4
  693.5 1.4 reshape.38
  694.9 2.5 fusion.21
  697.4 2.6 fusion.19
  700.0 12.7 %while.44 = (s32[]{:T(128)}, f32[256,16,12]{0,2,1:T(8,128)}, f32[256,16]{0,1:T(8,128)S(1)}, bf16[768,1024]{1,0:T(8,128)(2,1)}, bf16[192,768]{1,0:T(8,128)(2,1)S(...) while((s32[]{:T(128)}, f32[256,16,12]{0,2,1:T(8,128)}, ...), condition=%wide.region_8.0_spmd.clone, body=%wide.region_6.0_spmd.clone.sunk | while | flops 212013056 | bytes 2457774 | solution.py:85
  700.0 1.4 convolution_convert_fusion.2
  701.5 2.8 fusion.61
  704.3 1.4 convert_reduce_fusion.2
  705.8 1.5 convolution_convert_fusion.2
  707.3 3.9 fusion.61
  711.2 1.4 convert_reduce_fusion.2
  712.7 1.7 reshape.39
  714.3 250.5 %all-reduce.2 = f32[256,16]{0,1:T(8,128)S(1)} all-reduce(f32[256,16]{0,1:T(8,128)S(1)} %get-tuple-element.256), channel_id=4, replica_groups=mesh['dp'=64,'dim'=4] {'dp'}, use_global_device_ids=true, to_apply=%region_10.0.clone | all-reduce | flops 4096 | bytes 32768
  964.9 0.1 constant_dynamic-slice_fusion.2
  965.0 0.1 copy.13
  965.0 0.1 broadcast_in_dim.27
  965.1 0.1 reshape.40
  965.2 1.0 constant_dynamic-slice_fusion.3
  966.2 0.1 copy.14
  966.3 0.6 div.19
  (38 shorter events, 0.3 us)
Async XLA Ops:
  7.2 33.6 %all-gather.8.cloned.1.call-start = ((), (), s32[]{:S(2)}) async-start(), calls=%async_computation | async-start | bytes 1966080 | tf_op jit(solution)/shard_map/all_gather | solution.py:22
  7.9 223.9 %all-reduce.6.cloned.1.call-start = ((), (), s32[]{:S(2)}) async-start(), calls=%async_computation.2 | async-start | bytes 1179648
  40.8 7.7 copy-start.6
  41.5 2.1 copy-start
  44.9 2.1 copy-start
  47.5 0.8 copy-start.1
  48.4 291.8 %all-gather.10.cloned.1.call-start = ((), (), s32[]{:S(2)}) async-start(), calls=%async_computation.1 | async-start | bytes 3158016 | tf_op jit(solution)/shard_map/all_gather | solution.py:52
  340.2 5.0 copy-start.2
  351.4 109.1 %all-gather.12.cloned.1.call-start = ((), (), s32[]{:S(2)}) async-start(), calls=%async_computation.4 | async-start | bytes 3158016 | tf_op jit(solution)/shard_map/while/body/eval_jaxpr/all_gather | solution.py:52
  354.7 0.6 copy-start.3
  355.3 108.5 %copy-start.4 = (f32[3,768]{1,0:T(4,128)S(1)}, f32[3,768]{1,0:T(4,128)}, u32[]{:S(2)}) copy-start(f32[3,768]{1,0:T(4,128)} %copy-done.3) | copy-start | bytes 27652 | tf_op jit(solution)/shard_map/while
  463.9 109.1 %all-gather.12.cloned.1.call-start = ((), (), s32[]{:S(2)}) async-start(), calls=%async_computation.4 | async-start | bytes 3158016 | tf_op jit(solution)/shard_map/while/body/eval_jaxpr/all_gather | solution.py:52
  467.1 0.6 copy-start.3
  467.8 108.5 %copy-start.4 = (f32[3,768]{1,0:T(4,128)S(1)}, f32[3,768]{1,0:T(4,128)}, u32[]{:S(2)}) copy-start(f32[3,768]{1,0:T(4,128)} %copy-done.3) | copy-start | bytes 27652 | tf_op jit(solution)/shard_map/while
  576.3 109.1 %all-gather.12.cloned.1.call-start = ((), (), s32[]{:S(2)}) async-start(), calls=%async_computation.4 | async-start | bytes 3158016 | tf_op jit(solution)/shard_map/while/body/eval_jaxpr/all_gather | solution.py:52
  579.6 0.6 copy-start.3
  580.2 108.5 %copy-start.4 = (f32[3,768]{1,0:T(4,128)S(1)}, f32[3,768]{1,0:T(4,128)}, u32[]{:S(2)}) copy-start(f32[3,768]{1,0:T(4,128)} %copy-done.3) | copy-start | bytes 27652 | tf_op jit(solution)/shard_map/while
  688.7 276.6 %all-reduce.8.cloned.1.call-start = ((), (), s32[]{:S(2)}) async-start(), calls=%async_computation.3 | async-start | bytes 393216
  697.4 2.6 copy-start.5
Sparse Core Ops, SparseCore 0:
  9.8 30.9 all-gather.7
  48.5 183.2 all-reduce.5
  236.1 104.0 all-gather.9
  356.3 104.2 all-gather.11
  468.7 104.2 all-gather.11
  581.1 104.2 all-gather.11
  714.5 177.2 all-reduce.7
where the time goes:
time: 975 us; the launch traced here: 974 us
  waiting for transfers between devices  637 us (65%)
  blocking collectives  251 us (26%)
  local copies, waits for them, and re-layouts  29.5 us (3%)
  matrix products  29.4 us (3%)
  between operations  16 us (2%)
  other arithmetic  10.7 us (1%)
    all_gather x4, waiting for transfers between devices, gather_spread(): return lax.all_gather(rows, ('dp', 'dim'), axis=0, tiled=True)  422 us
    unnamed x1, blocking collectives  251 us
    unnamed x6, waiting for transfers between devices  183 us
    all_gather x1, waiting for transfers between devices, per_device(): gathered_rows = lax.all_gather(vectors, 'dim', axis=0, tiled=True)  31.9 us
  transfers between devices with their start and end apart: 7, of which 6 were waited for; matrix products, arithmetic and copies ran while one was open for 0% of the time, Pallas kernels for 0%

commit v1 on v0

--- a/solution.py
+++ b/solution.py
@@ -49,7 +49,10 @@
     dim_index = lax.axis_index("dim")
 
     def gather_spread(rows):
-        return lax.all_gather(rows, ("dp", "dim"), axis=0, tiled=True)
+        return jnp.concatenate(
+            lax.all_to_all(jnp.stack([rows] * lax.axis_size(("dp", "dim"))), ("dp", "dim"), 0, 0),
+            axis=0,
+        )
 
     gathered = gather_spread(own_rows)
     magnitude = jnp.sqrt(jnp.sum(gathered * gathered))

time: 975 us -> 891 us (0.914)
  waiting for transfers between devices: 637 us -> 520 us
  starting transfers between devices: 0.28 us -> 34.5 us
    all_gather x4 -> x0, waiting for transfers between devices: 422 us -> none  [gather_spread(): return lax.all_gather(rows, ('dp', 'dim'), axis=0, tiled=True)]
    all_to_all x0 -> x4, waiting for transfers between devices: none -> 305 us  [gather_spread(): lax.all_to_all(jnp.stack([rows] * lax.axis_size(('dp', 'dim'))), ('dp', '...]
    all_to_all x0 -> x4, starting transfers between devices: none -> 34.3 us  [gather_spread(): lax.all_to_all(jnp.stack([rows] * lax.axis_size(('dp', 'dim'))), ('dp', '...]
    while x19 -> x4, local copies, waits for them, and re-layouts: 11.5 us -> 0.01 us
    unnamed x6 -> x5, waiting for transfers between devices: 183 us -> 183 us
where the time goes in v1:
time: 891 us; the launch traced here: 890 us
  waiting for transfers between devices  520 us (58%)
  blocking collectives  246 us (28%)
  local copies, waits for them, and re-layouts  35.4 us (4%)
  starting transfers between devices  34.5 us (4%)
  matrix products  29.4 us (3%)
  between operations  15.7 us (2%)
    all_to_all x4, waiting for transfers between devices, gather_spread(): lax.all_to_all(jnp.stack([rows] * lax.axis_size(('dp', 'dim'))), ('dp', '...  305 us
    unnamed x1, blocking collectives  246 us
    unnamed x5, waiting for transfers between devices  183 us
    all_to_all x4, starting transfers between devices, gather_spread(): lax.all_to_all(jnp.stack([rows] * lax.axis_size(('dp', 'dim'))), ('dp', '...  34.3 us
    all_gather x1, waiting for transfers between devices, per_device(): gathered_rows = lax.all_gather(vectors, 'dim', axis=0, tiled=True)  31.9 us
  transfers between devices with their start and end apart: 7, of which 6 were waited for; matrix products, arithmetic and copies ran while one was open for 0% of the time, Pallas kernels for 0%

profile of v1, /device:TPU:8, one launch (start us, length us, event | category | flops | bytes accessed | tf_op | source)
XLA Modules:
  0.0 889.7 jit_solution(16600456956071933018)
XLA Ops:
  7.2 0.7 all-gather.2.cloned.1.call-update
  8.0 0.9 reshape.46
  8.9 31.9 %all-gather.2.cloned.1.call-done = bf16[768,1024]{1,0:T(8,128)(2,1)} async-done(((bf16[192,1024]{1,0:T(8,128)(2,1)}), bf16[768,1024]{1,0:T(8,128)(2,1)}) %all-gather.2.cloned.1.call-update) | async-done | bytes 1572880 | tf_op jit(solution)/shard_map/all_gather | solution.py:22
  40.8 6.8 while.43
  40.8 0.8 constant_dynamic-slice_fusion.8
  41.5 2.0 fusion.57
  43.5 0.1 convert_element_type.62
  43.6 0.5 convolution_add_fusion.2
  44.2 0.8 constant_dynamic-slice_fusion.8
  44.9 2.0 fusion.57
  46.9 0.1 convert_element_type.62
  47.0 0.5 convolution_add_fusion.2
  47.6 0.8 copy-done.1
  48.4 0.6 dynamic-slice
  49.6 182.2 %all-reduce.6.cloned.1.call-done = f32[192,768]{1,0:T(8,128)} async-done(((f32[192,768]{1,0:T(8,128)}), f32[192,768]{1,0:T(8,128)}) %all-reduce.6.cloned.1.call-update) | async-done | bytes 589840
  231.8 0.8 constant_dynamic-slice_fusion.4
  232.6 2.1 stack.4
  234.7 10.5 %all-to-all-start.1 = ((f32[256,3,768]{2,1,0:T(4,128)}), f32[256,3,768]{2,1,0:T(4,128)S(1)}, u32[]{:S(2)}, u32[]{:S(2)}) async-start(f32[256,3,768]{2,1,0:T(4,128)} %stack.4), calls=%async_computation.1 | async-start | bytes 6291456 | tf_op jit(solution)/shard_map/all_to_all | solution.py:53
  245.1 0.0 all-reduce.8.cloned.1.call-start
  245.8 76.2 %all-to-all-done.1 = f32[256,3,768]{2,1,0:T(4,128)S(1)} async-done(((f32[256,3,768]{2,1,0:T(4,128)}), f32[256,3,768]{2,1,0:T(4,128)S(1)}, u32[]{:S(2)}, u32[]{:S(2)}) %all-to-all-start.1) | async-done | bytes 2359328 | tf_op jit(solution)/shard_map/all_to_all | solution.py:53
  322.0 2.2 multiply_reduce_fusion
  324.9 2.2 broadcast_divide_fusion
  327.1 3.2 div.22
  330.4 0.8 broadcast_divide_fusion.1
  331.2 278.2 %while.42 = (s32[]{:T(128)}, f32[3,768]{1,0:T(4,128)S(1)}, f32[768,768]{1,0:T(8,128)S(1)}, s32[]{:T(128)}) while((s32[]{:T(128)}, f32[3,768]{1,0:T(4,128)S(1)}, f32[768,768]{1,0:T(8,128)S(1)}, s32[]{:T(128)}) %tuple.81), condition=%wide.region_5.0_spmd, body=%wide.region_4.0_spmd.sunk | while | flops 42474240 | bytes 20502612 | solution.py:67
  331.2 2.0 fusion.52
  333.2 1.2 fusion.53
  334.4 2.1 stack.6
  336.5 8.0 all-to-all-start
  344.5 76.2 %all-to-all-done = f32[256,3,768]{2,1,0:T(4,128)} async-done(((f32[256,3,768]{2,1,0:T(4,128)}), f32[256,3,768]{2,1,0:T(4,128)}, u32[]{:S(2)}, u32[]{:S(2)}) %all-to-all-start) | async-done | bytes 2359328 | tf_op jit(solution)/shard_map/while/body/eval_jaxpr/all_to_all | solution.py:53
  420.6 3.2 reshape.61
  423.9 2.0 fusion.52
  425.9 1.2 fusion.53
  427.1 2.1 stack.6
  429.2 8.0 all-to-all-start
  437.2 76.2 %all-to-all-done = f32[256,3,768]{2,1,0:T(4,128)} async-done(((f32[256,3,768]{2,1,0:T(4,128)}), f32[256,3,768]{2,1,0:T(4,128)}, u32[]{:S(2)}, u32[]{:S(2)}) %all-to-all-start) | async-done | bytes 2359328 | tf_op jit(solution)/shard_map/while/body/eval_jaxpr/all_to_all | solution.py:53
  513.4 3.2 reshape.61
  516.6 2.0 fusion.52
  518.6 1.2 fusion.53
  519.9 2.1 stack.6
  522.0 8.0 all-to-all-start
  529.9 76.2 %all-to-all-done = f32[256,3,768]{2,1,0:T(4,128)} async-done(((f32[256,3,768]{2,1,0:T(4,128)}), f32[256,3,768]{2,1,0:T(4,128)}, u32[]{:S(2)}, u32[]{:S(2)}) %all-to-all-start) | async-done | bytes 2359328 | tf_op jit(solution)/shard_map/while/body/eval_jaxpr/all_to_all | solution.py:53
  606.1 3.2 reshape.61
  609.4 2.6 reshape.47
  611.9 2.1 constant_dynamic-slice_fusion.5
  614.1 1.4 reshape.48
  615.5 2.5 fusion.21
  618.0 2.6 fusion.19
  620.6 12.7 %while.44 = (s32[]{:T(128)}, f32[256,16,12]{0,2,1:T(8,128)}, f32[256,16]{0,1:T(8,128)S(1)}, bf16[768,1024]{1,0:T(8,128)(2,1)}, bf16[192,768]{1,0:T(8,128)(2,1)S(...) while((s32[]{:T(128)}, f32[256,16,12]{0,2,1:T(8,128)}, ...), condition=%wide.region_8.0_spmd.clone, body=%wide.region_6.0_spmd.clone.sunk | while | flops 212013056 | bytes 2457766 | solution.py:88
  620.6 1.5 convolution_convert_fusion.2
  622.1 2.8 fusion.61
  624.9 1.4 convert_reduce_fusion.2
  626.4 1.5 convolution_convert_fusion.2
  627.9 3.9 fusion.61
  631.9 1.4 convert_reduce_fusion.2
  633.3 1.6 reshape.49
  635.0 246.2 %all-reduce.2 = f32[256,16]{0,1:T(8,128)S(1)} all-reduce(f32[256,16]{0,1:T(8,128)S(1)} %get-tuple-element.256), channel_id=4, replica_groups=mesh['dp'=64,'dim'=4] {'dp'}, use_global_device_ids=true, to_apply=%region_10.0.clone | all-reduce | flops 4096 | bytes 32768
  881.1 0.1 constant_dynamic-slice_fusion.2
  881.2 0.1 copy.13
  881.3 0.1 broadcast_in_dim.27
  881.4 0.1 reshape.50
  881.5 1.0 constant_dynamic-slice_fusion.3
  882.5 0.1 copy.14
  882.6 0.6 div.23
  (24 shorter events, 0.3 us)
Async XLA Ops:
  7.2 33.6 %all-gather.2.cloned.1.call-start = ((), (), s32[]{:S(2)}) async-start(), calls=%async_computation.2 | async-start | bytes 1966080 | tf_op jit(solution)/shard_map/all_gather | solution.py:22
  7.9 223.9 %all-reduce.6.cloned.1.call-start = ((), (), s32[]{:S(2)}) async-start(), calls=%async_computation.3 | async-start | bytes 1179648
  40.8 7.6 copy-start.3
  41.5 2.1 copy-start
  44.9 2.1 copy-start
  47.5 0.8 copy-start.1
  234.7 87.4 %all-to-all-start.1 = ((f32[256,3,768]{2,1,0:T(4,128)}), f32[256,3,768]{2,1,0:T(4,128)S(1)}, u32[]{:S(2)}, u32[]{:S(2)}) async-start(f32[256,3,768]{2,1,0:T(4,128)} %stack.4), calls=%async_computation.1 | async-start | bytes 6291456 | tf_op jit(solution)/shard_map/all_to_all | solution.py:53
  245.1 636.4 %all-reduce.8.cloned.1.call-start = ((), (), s32[]{:S(2)}) async-start(), calls=%async_computation.4 | async-start | bytes 393216
  336.5 84.1 %all-to-all-start = ((f32[256,3,768]{2,1,0:T(4,128)}), f32[256,3,768]{2,1,0:T(4,128)}, u32[]{:S(2)}, u32[]{:S(2)}) async-start(f32[256,3,768]{2,1,0:T(4,128)} %stack.6), calls=%async_computation | async-start | bytes 6291456 | tf_op jit(solution)/shard_map/while/body/eval_jaxpr/all_to_all | solution.py:53
  429.2 84.1 %all-to-all-start = ((f32[256,3,768]{2,1,0:T(4,128)}), f32[256,3,768]{2,1,0:T(4,128)}, u32[]{:S(2)}, u32[]{:S(2)}) async-start(f32[256,3,768]{2,1,0:T(4,128)} %stack.6), calls=%async_computation | async-start | bytes 6291456 | tf_op jit(solution)/shard_map/while/body/eval_jaxpr/all_to_all | solution.py:53
  522.0 84.1 %all-to-all-start = ((f32[256,3,768]{2,1,0:T(4,128)}), f32[256,3,768]{2,1,0:T(4,128)}, u32[]{:S(2)}, u32[]{:S(2)}) async-start(f32[256,3,768]{2,1,0:T(4,128)} %stack.6), calls=%async_computation | async-start | bytes 6291456 | tf_op jit(solution)/shard_map/while/body/eval_jaxpr/all_to_all | solution.py:53
  618.0 2.6 copy-start.2
Sparse Core Ops, SparseCore 0:
  9.8 30.9 all-gather.1
  48.5 183.2 all-reduce.5
  635.1 171.8 all-reduce.7
